TPU v7x, 32 devices: a whole 2x2x4 slice. The times are simulated.
32 devices in a mesh: enc: 4 (over z), dp: 8 (over y, x, core).
Axes of the slice: x: 2, y: 2, z: 4, core: 2. Of those that a mesh axis runs over, the one named last changes fastest.
Arguments:
- text: bfloat16 [16384, 768], P(('enc', 'dp')), may hold values from -6 to 6
- region_feats: bfloat16 [13312, 2048], P(('enc', 'dp')), may hold values from -6 to 6
- boxes: bfloat16 [4, 13312], P(None, ('enc', 'dp')), may hold values from 0 to 1
- caption_count: int32 [128], P(('enc', 'dp')), may hold values from 8 to 128, as said below
- region_count: int32 [128], P(('enc', 'dp')), may hold values from 36 to 100, as said below
- region_offset: int32 [32], P(('enc', 'dp')), may hold values from 0 to 31
- w_img: bfloat16 [2048, 768], P(('enc', 'dp')), may hold values from -0.125 to 0.125
- w_box: bfloat16 [4, 768], replicated, may hold values from -3 to 3
- b_img: float32 [768], replicated, may hold values from -3 to 3
- g_reg: float32 [768], replicated, may hold values from 0.25 to 1.75
- beta_reg: float32 [768], replicated, may hold values from -1.75 to 1.75
- w_query: bfloat16 [768, 768], P(('enc', 'dp')), may hold values from -0.21875 to 0.21875
- b_query: float32 [768], replicated, may hold values from -1.75 to 1.75
- w_key: bfloat16 [768, 768], P(('enc', 'dp')), may hold values from -0.21875 to 0.21875
- w_value: bfloat16 [768, 768], P(('enc', 'dp')), may hold values from -0.21875 to 0.21875
- b_value: float32 [768], replicated, may hold values from -1.75 to 1.75
- w_out: bfloat16 [768, 768], P(('enc', 'dp')), may hold values from -1.75 to 1.75
- b_out: float32 [768], replicated, may hold values from -1.75 to 1.75
- g_one: float32 [768], replicated, may hold values from 0.25 to 1.75
- beta_one: float32 [768], replicated, may hold values from -1.75 to 1.75
- w_up: bfloat16 [768, 3072], P(('enc', 'dp')), may hold values from -0.21875 to 0.21875
- b_up: float32 [3072], replicated, may hold values from -1.75 to 1.75
- w_down: bfloat16 [3072, 768], P(('enc', 'dp')), may hold values from -0.109375 to 0.109375
- b_down: float32 [768], replicated, may hold values from -1.75 to 1.75
- g_two: float32 [768], replicated, may hold values from 0.25 to 1.75
- beta_two: float32 [768], replicated, may hold values from -1.75 to 1.75
- cotangent: bfloat16 [32768, 768], P(('enc', 'dp'))
Outputs:
- output: bfloat16 [32768, 768], P(('enc', 'dp'))
- grad_text: bfloat16 [16384, 768], P(('enc', 'dp'))
- grad_feats: bfloat16 [13312, 2048], P(('enc', 'dp'))
- grad_boxes: bfloat16 [4, 13312], P(None, ('enc', 'dp'))
- grad_w_img: float32 [2048, 768], replicated
- grad_w_box: float32 [4, 768], replicated
- grad_b_img: float32 [768], replicated
- grad_g_reg: float32 [768], replicated
- grad_beta_reg: float32 [768], replicated
- grad_w_query: float32 [768, 768], replicated
- grad_b_query: float32 [768], replicated
- grad_w_key: float32 [768, 768], replicated
- grad_w_value: float32 [768, 768], replicated
- grad_b_value: float32 [768], replicated
- grad_w_out: float32 [768, 768], replicated
- grad_b_out: float32 [768], replicated
- grad_g_one: float32 [768], replicated
- grad_beta_one: float32 [768], replicated
- grad_w_up: float32 [768, 3072], replicated
- grad_b_up: float32 [3072], replicated
- grad_w_down: float32 [3072, 768], replicated
- grad_b_down: float32 [768], replicated
- grad_g_two: float32 [768], replicated
- grad_beta_two: float32 [768], replicated
Inputs may be any that keep to these rules, and one draw needn't show every extreme that they name: `caption_count`: some sequence has exactly 128 caption tokens. `region_count`: in every draw some holder's 4 sequences all have 100 regions.
All inputs are finite; a program needn't handle non-finite values.
Results may differ from a plain program's by a relative error of at most 0.018.
Values may be sent and summed in bfloat16 or wider, within the bound.
No kernel may reach another device: no remote copies, remote signals or barrier semaphores. Data moves between devices by JAX's collectives and lax.ppermute only.
A program may use at most 192 MiB of HBM per device.

v0:
```python
import jax
import jax.numpy as jnp
from jax import lax
from jax.sharding import PartitionSpec as P

HEADS = 12
epsilon = 1e-05


def normalize(values, gain_vec, shift_vec):
    centered = values - jnp.mean(values, -1, keepdims=True)
    inverse = lax.rsqrt(jnp.mean(centered * centered, -1, keepdims=True) + epsilon)
    normed = centered * inverse
    return (normed * gain_vec + shift_vec, normed, inverse)


def normalize_back(upstream, normed, inverse, gain_vec):
    weighted = upstream * gain_vec
    result = inverse * (
        weighted
        - jnp.mean(weighted, -1, keepdims=True)
        - normed * jnp.mean(weighted * normed, -1, keepdims=True)
    )
    return (result, jnp.sum(upstream * normed, 0), jnp.sum(upstream, 0))


def exact_gelu(values):
    return jax.nn.gelu(values, approximate=False)


def outer_sum(row_data, row_grad):
    return jnp.einsum("ra,rb->ab", row_data, row_grad, preferred_element_type=jnp.float32)


def back_product(row_grad, weight):
    return jnp.einsum("rb,ab->ra", row_grad, weight, preferred_element_type=jnp.float32)


def column_sum(row_grad):
    return jnp.sum(row_grad.astype(jnp.float32), 0)


def body(
    text,
    region_feats,
    boxes,
    caption_count,
    region_count,
    region_offset,
    w_img,
    w_box,
    b_img,
    g_reg,
    beta_reg,
    w_query,
    b_query,
    w_key,
    w_value,
    b_value,
    w_out,
    b_out,
    g_one,
    beta_one,
    w_up,
    b_up,
    w_down,
    b_down,
    g_two,
    beta_two,
    cotangent,
):
    img_full, query_full, key_full, value_full, out_full, up_full, down_full = (
        lax.all_gather(w_img, ("enc", "dp"), axis=0, tiled=True),
        lax.all_gather(w_query, ("enc", "dp"), axis=0, tiled=True),
        lax.all_gather(w_key, ("enc", "dp"), axis=0, tiled=True),
        lax.all_gather(w_value, ("enc", "dp"), axis=0, tiled=True),
        lax.all_gather(w_out, ("enc", "dp"), axis=0, tiled=True),
        lax.all_gather(w_up, ("enc", "dp"), axis=0, tiled=True),
        lax.all_gather(w_down, ("enc", "dp"), axis=0, tiled=True),
    )
    device_count = lax.axis_size(("enc", "dp"))
    seq_count = caption_count.shape[0]
    model_width = text.shape[1]
    text_len = text.shape[0] // seq_count
    seq_len = cotangent.shape[0] // seq_count
    region_len = seq_len - text_len
    sent_rows = region_feats.shape[0]
    per_peer = sent_rows // device_count
    head_dim = model_width // HEADS
    score_scale = head_dim ** (-0.5)
    pre_norm = (
        jnp.dot(region_feats, img_full, preferred_element_type=jnp.float32)
        + jnp.einsum("cr,cd->rd", boxes, w_box, preferred_element_type=jnp.float32)
        + b_img
    )
    encoded, enc_normed, enc_inverse = normalize(pre_norm, g_reg, beta_reg)
    received = lax.all_to_all(
        encoded.astype(jnp.bfloat16), ("enc", "dp"), split_axis=0, concat_axis=0, tiled=True
    )
    position = jnp.arange(sent_rows, dtype=jnp.int32)
    arrival = (
        position % per_peer * device_count
        + (position // per_peer - region_offset[0]) % device_count
    )
    starts = jnp.cumsum(region_count) - region_count
    slot_total = seq_count * region_len
    slot_pos = jnp.arange(slot_total, dtype=jnp.int32) % region_len
    wanted = jnp.repeat(starts, region_len, total_repeat_length=slot_total) + slot_pos
    slot_live = slot_pos < jnp.repeat(region_count, region_len, total_repeat_length=slot_total)
    placement = ((wanted[:, None] == arrival[None, :]) & slot_live[:, None]).astype(jnp.bfloat16)
    regions = jnp.dot(placement, received, preferred_element_type=jnp.float32).astype(jnp.bfloat16)
    hidden_in = jnp.concatenate(
        [
            text.reshape(seq_count, text_len, model_width),
            regions.reshape(seq_count, region_len, model_width),
        ],
        1,
    ).reshape(seq_count * seq_len, model_width)
    key_live = jnp.concatenate(
        [
            jnp.arange(text_len)[None, :] < caption_count[:, None],
            jnp.arange(region_len)[None, :] < region_count[:, None],
        ],
        1,
    )
    row_live = key_live.reshape(-1, 1).astype(jnp.float32)

    def heads_view(tensor):
        return tensor.reshape(seq_count, seq_len, HEADS, head_dim)

    query_heads = heads_view(
        (jnp.dot(hidden_in, query_full, preferred_element_type=jnp.float32) + b_query).astype(
            jnp.bfloat16
        )
    )
    key_heads = heads_view(
        jnp.dot(hidden_in, key_full, preferred_element_type=jnp.float32).astype(jnp.bfloat16)
    )
    value_heads = heads_view(
        (jnp.dot(hidden_in, value_full, preferred_element_type=jnp.float32) + b_value).astype(
            jnp.bfloat16
        )
    )
    scores = (
        jnp.einsum("sqhd,skhd->shqk", query_heads, key_heads, preferred_element_type=jnp.float32)
        * score_scale
    )
    scores = jnp.where(key_live[:, None, None, :], scores, -1e30)
    row_max = jnp.max(scores, -1, keepdims=True)
    exp_scores = jnp.exp(scores - row_max)
    attn_probs = exp_scores / jnp.sum(exp_scores, -1, keepdims=True)
    probs_low = attn_probs.astype(jnp.bfloat16)
    context = (
        jnp.einsum("shqk,skhd->sqhd", probs_low, value_heads, preferred_element_type=jnp.float32)
        .reshape(-1, model_width)
        .astype(jnp.bfloat16)
    )
    mixed = (
        hidden_in.astype(jnp.float32)
        + jnp.dot(context, out_full, preferred_element_type=jnp.float32)
        + b_out
    )
    normed_one, one_normed, one_inverse = normalize(mixed, g_one, beta_one)
    normed_one = normed_one.astype(jnp.bfloat16)
    gate_in = jnp.dot(normed_one, up_full, preferred_element_type=jnp.float32) + b_up
    activated = exact_gelu(gate_in).astype(jnp.bfloat16)
    second_in = (
        normed_one.astype(jnp.float32)
        + jnp.dot(activated, down_full, preferred_element_type=jnp.float32)
        + b_down
    )
    normed_two, two_normed, two_inverse = normalize(second_in, g_two, beta_two)
    output = (normed_two * row_live).astype(jnp.bfloat16)
    grad_second = cotangent.astype(jnp.float32) * row_live
    grad_second_in, grad_g_two, grad_beta_two = normalize_back(
        grad_second, two_normed, two_inverse, g_two
    )
    grad_down_out = grad_second_in.astype(jnp.bfloat16)
    grad_w_down = outer_sum(activated, grad_down_out)
    grad_b_down = column_sum(grad_down_out)
    grad_activated = back_product(grad_down_out, down_full)
    gelu_pull = jax.vjp(exact_gelu, gate_in)[1]
    grad_gate = gelu_pull(grad_activated)[0].astype(jnp.bfloat16)
    grad_w_up = outer_sum(normed_one, grad_gate)
    grad_b_up = column_sum(grad_gate)
    grad_first = back_product(grad_gate, up_full) + grad_second_in
    grad_mixed, grad_g_one, grad_beta_one = normalize_back(
        grad_first, one_normed, one_inverse, g_one
    )
    grad_attn = grad_mixed.astype(jnp.bfloat16)
    grad_w_out = outer_sum(context, grad_attn)
    grad_b_out = column_sum(grad_attn)
    grad_context = heads_view(back_product(grad_attn, out_full).astype(jnp.bfloat16))
    grad_probs = jnp.einsum(
        "sqhd,skhd->shqk", grad_context, value_heads, preferred_element_type=jnp.float32
    )
    grad_values = (
        jnp.einsum("shqk,sqhd->skhd", probs_low, grad_context, preferred_element_type=jnp.float32)
        .reshape(-1, model_width)
        .astype(jnp.bfloat16)
    )
    grad_scores = (
        attn_probs * (grad_probs - jnp.sum(attn_probs * grad_probs, -1, keepdims=True))
    ).astype(jnp.bfloat16)
    grad_query = (
        (
            jnp.einsum(
                "shqk,skhd->sqhd", grad_scores, key_heads, preferred_element_type=jnp.float32
            )
            * score_scale
        )
        .reshape(-1, model_width)
        .astype(jnp.bfloat16)
    )
    grad_keys = (
        (
            jnp.einsum(
                "shqk,sqhd->skhd", grad_scores, query_heads, preferred_element_type=jnp.float32
            )
            * score_scale
        )
        .reshape(-1, model_width)
        .astype(jnp.bfloat16)
    )
    grad_w_query = outer_sum(hidden_in, grad_query)
    grad_b_query = column_sum(grad_query)
    grad_w_key = outer_sum(hidden_in, grad_keys)
    grad_w_value = outer_sum(hidden_in, grad_values)
    grad_b_value = column_sum(grad_values)
    grad_hidden = (
        grad_mixed
        + back_product(grad_query, query_full)
        + back_product(grad_keys, key_full)
        + back_product(grad_values, value_full)
    )
    grad_hidden = grad_hidden.reshape(seq_count, seq_len, model_width)
    grad_text = grad_hidden[:, :text_len].reshape(-1, model_width).astype(jnp.bfloat16)
    grad_slots = grad_hidden[:, text_len:].reshape(-1, model_width).astype(jnp.bfloat16)
    grad_sent = jnp.einsum(
        "tn,td->nd", placement, grad_slots, preferred_element_type=jnp.float32
    ).astype(jnp.bfloat16)
    grad_encoded = lax.all_to_all(
        grad_sent, ("enc", "dp"), split_axis=0, concat_axis=0, tiled=True
    ).astype(jnp.float32)
    grad_pre, grad_g_reg, grad_beta_reg = normalize_back(
        grad_encoded, enc_normed, enc_inverse, g_reg
    )
    grad_pre = grad_pre.astype(jnp.bfloat16)
    grad_w_img = outer_sum(region_feats, grad_pre)
    grad_w_box = jnp.einsum("cr,rd->cd", boxes, grad_pre, preferred_element_type=jnp.float32)
    grad_b_img = column_sum(grad_pre)
    grad_feats = back_product(grad_pre, img_full).astype(jnp.bfloat16)
    grad_boxes = jnp.einsum(
        "cd,rd->cr", w_box, grad_pre, preferred_element_type=jnp.float32
    ).astype(jnp.bfloat16)
    (
        grad_w_img,
        grad_w_box,
        grad_b_img,
        grad_g_reg,
        grad_beta_reg,
        grad_w_query,
        grad_b_query,
        grad_w_key,
        grad_w_value,
        grad_b_value,
        grad_w_out,
        grad_b_out,
        grad_g_one,
        grad_beta_one,
        grad_w_up,
        grad_b_up,
        grad_w_down,
        grad_b_down,
        grad_g_two,
        grad_beta_two,
    ) = lax.psum(
        (
            grad_w_img,
            grad_w_box,
            grad_b_img,
            grad_g_reg,
            grad_beta_reg,
            grad_w_query,
            grad_b_query,
            grad_w_key,
            grad_w_value,
            grad_b_value,
            grad_w_out,
            grad_b_out,
            grad_g_one,
            grad_beta_one,
            grad_w_up,
            grad_b_up,
            grad_w_down,
            grad_b_down,
            grad_g_two,
            grad_beta_two,
        ),
        ("enc", "dp"),
    )
    return (
        output,
        grad_text,
        grad_feats,
        grad_boxes,
        grad_w_img,
        grad_w_box,
        grad_b_img,
        grad_g_reg,
        grad_beta_reg,
        grad_w_query,
        grad_b_query,
        grad_w_key,
        grad_w_value,
        grad_b_value,
        grad_w_out,
        grad_b_out,
        grad_g_one,
        grad_beta_one,
        grad_w_up,
        grad_b_up,
        grad_w_down,
        grad_b_down,
        grad_g_two,
        grad_beta_two,
    )


def solution(mesh):
    return jax.shard_map(
        body,
        mesh=mesh,
        in_specs=(
            P(("enc", "dp"), None),
            P(("enc", "dp"), None),
            P(None, ("enc", "dp")),
            P(("enc", "dp")),
            P(("enc", "dp")),
            P(("enc", "dp")),
            P(("enc", "dp"), None),
            P(),
            P(),
            P(),
            P(),
            P(("enc", "dp"), None),
            P(),
            P(("enc", "dp"), None),
            P(("enc", "dp"), None),
            P(),
            P(("enc", "dp"), None),
            P(),
            P(),
            P(),
            P(("enc", "dp"), None),
            P(),
            P(("enc", "dp"), None),
            P(),
            P(),
            P(),
            P(("enc", "dp"), None),
        ),
        out_specs=(
            P(("enc", "dp"), None),
            P(("enc", "dp"), None),
            P(("enc", "dp"), None),
            P(None, ("enc", "dp")),
            P(),
            P(),
            P(),
            P(),
            P(),
            P(),
            P(),
            P(),
            P(),
            P(),
            P(),
            P(),
            P(),
            P(),
            P(),
            P(),
            P(),
            P(),
            P(),
            P(),
        ),
        check_vma=False,
    )
```

profile of v0, /device:TPU:0, one launch (start us, length us, event | category | flops | bytes accessed | tf_op | source)
XLA Modules:
  0.0 1141.4 jit_solution(5793821062588575223)
XLA Ops:
  11.2 61.4 %all-gather.8.cloned.1.call-done = bf16[2048,768]{1,0:T(8,128)(2,1)} async-done(((bf16[64,768]{1,0:T(8,128)(2,1)}), bf16[2048,768]{1,0:T(8,128)(2,1)}) %all-gather.8.cloned.1.call-update) | async-done | bytes 3145744 | tf_op jit(solution)/shard_map/all_gather | solution.py:73
  72.6 3.4 fusion.82
  79.5 3.4 all-to-all-start
  85.8 2.6 select_compare_fusion
  89.0 2.6 select_add_fusion
  91.7 12.7 %all-to-all-done = bf16[32,13,768]{2,1,0:T(8,128)(2,1)S(1)} async-done(((bf16[32,13,768]{2,1,0:T(8,128)(2,1)}), bf16[32,13,768]{2,1,0:T(8,128)(2,1)S(1)}, u32[]{:S(2)}, u32[]{:S(2)}) %all-to-all-start) | async-done | bytes 639008 | tf_op jit(solution)/shard_map/all_to_all | solution.py:97
  106.5 24.1 %all-gather.14.cloned.1.call-done = bf16[768,768]{1,0:T(8,128)(2,1)} async-done(((bf16[24,768]{1,0:T(8,128)(2,1)}), bf16[768,768]{1,0:T(8,128)(2,1)}) %all-gather.14.cloned.1.call-update) | async-done | bytes 1179664 | tf_op jit(solution)/shard_map/all_gather | solution.py:75
  130.7 3.8 convolution_convert_fusion.2
  134.5 1.7 copy.66
  136.2 2.4 reshape.314
  138.6 48.0 %all-gather.12.cloned.1.call-done = bf16[768,768]{1,0:T(8,128)(2,1)} async-done(((bf16[24,768]{1,0:T(8,128)(2,1)}), bf16[768,768]{1,0:T(8,128)(2,1)}) %all-gather.12.cloned.1.call-update) | async-done | bytes 1179664 | tf_op jit(solution)/shard_map/all_gather | solution.py:74
  186.6 3.1 add_convert_fusion.3
  189.7 1.6 copy.65
  191.4 2.9 reshape.313
  194.3 48.1 %all-gather.10.cloned.1.call-done = bf16[768,768]{1,0:T(8,128)(2,1)} async-done(((bf16[24,768]{1,0:T(8,128)(2,1)}), bf16[768,768]{1,0:T(8,128)(2,1)}) %all-gather.10.cloned.1.call-update) | async-done | bytes 1179664 | tf_op jit(solution)/shard_map/all_gather | solution.py:76
  242.3 4.3 add_convert_fusion.4
  246.6 2.6 copy.64
  249.2 3.9 reshape.312
  253.0 7.8 fusion.39
  260.8 12.9 %fusion.78 = (f32[4,12,256]{2,1,0:T(8,128)S(1)}, f32[4,12,256,256]{2,3,1,0:T(8,128)S(1)}) fusion(f32[4,12,256,256]{2,3,1,0:T(8,128)} %fusion.39, pred[4,256]{1,0:T(4,128)(4,1)S(1)} %get-tuple-element.137), kind=kOutput, calls=%fused_computation.163 | output fusion | flops 18874624 | bytes 25216000 | tf_op jit(solution)/shard_map/sub | solution.py:150
  274.9 3.4 copy-done.8
  279.7 1.5 copy.89
  281.2 16.9 %all-gather.16.cloned.1.call-done = bf16[768,768]{1,0:T(8,128)(2,1)} async-done(((bf16[24,768]{1,0:T(8,128)(2,1)}), bf16[768,768]{1,0:T(8,128)(2,1)}) %all-gather.16.cloned.1.call-update) | async-done | bytes 1179664 | tf_op jit(solution)/shard_map/all_gather | solution.py:77
  298.1 3.4 fusion.79
  301.6 1.6 copy-done.3
  303.8 59.7 %all-gather.18.cloned.1.call-done = bf16[768,3072]{1,0:T(8,128)(2,1)} async-done(((bf16[24,3072]{1,0:T(8,128)(2,1)}), bf16[768,3072]{1,0:T(8,128)(2,1)}) %all-gather.18.cloned.1.call-update) | async-done | bytes 4718608 | tf_op jit(solution)/shard_map/all_gather | solution.py:78
  363.4 38.1 %multiply_convert_fusion.1 = (bf16[1024,3072]{1,0:T(8,128)(2,1)}, f32[1024,3072]{1,0:T(8,128)}, f32[1024,3072]{1,0:T(8,128)}) fusion(f32[3072]{0:T(1024)S(1)} %copy-done.60, bf16[768,3072]{1,0:T(8,128)(2,1)} %all-gather.18.cloned.1.call-done, f32[1024,768]{1,0:T(8,128)} %copy-done.3, f32[768]{0:T(1024)S(1)} %copy-done.34, f32[768]{0:T(1024)S(1)} %copy-done.29, ...), kind=kOutput, calls=%fused_computation.7 | convolution fusion | flops 5043388416 | bytes 39348224 | tf_op jit(solution)/shard_map/dot_general | solution.py:165
  401.5 27.3 %all-gather.20.cloned.1.call-done = bf16[3072,768]{1,0:T(8,128)(2,1)} async-done(((bf16[96,768]{1,0:T(8,128)(2,1)}), bf16[3072,768]{1,0:T(8,128)(2,1)}) %all-gather.20.cloned.1.call-update) | async-done | bytes 4718608 | tf_op jit(solution)/shard_map/all_gather | solution.py:79
  428.8 9.3 fusion.80
  439.6 2.4 multiply_reduce_fusion.1
  442.0 3.7 convert_reduce_fusion.1
  445.8 7.8 fusion.68
  453.6 18.8 %convert_reduce_fusion = (f32[3072]{0:T(1024)S(1)}, bf16[1024,3072]{1,0:T(8,128)(2,1)}) fusion(f32[1024,3072]{1,0:T(8,128)} %get-tuple-element.132, bf16[3072,768]{1,0:T(8,128)(2,1)} %all-gather.20.cloned.1.call-done, f32[1024,768]{1,0:T(8,128)} %copy-done.15, f32[1024,3072]{1,0:T(8,128)} %get-tuple-element.152, f32[3072]{0:T(1024)S(1)} %copy-done.60), kind=kOutput, calls=%fused_computation.3 | convolution fusion | flops 4886098944 | bytes 39346176 | tf_op jit(solution)/shard_map/rb,ab->ra/dot_general | solution.py:36
  472.4 10.1 multiply_reduce_fusion.2
  483.9 2.8 fusion.65
  486.7 2.6 convolution_convert_fusion.1
  489.3 1.7 copy.72
  491.1 2.4 reshape.315
  493.4 7.3 convert_reduce_fusion.3
  500.8 8.9 multiply_reduce_fusion
  509.7 6.9 multiply_convert_fusion
  516.7 2.0 fusion.31
  521.6 2.9 fusion.87
  527.6 2.9 fusion.85
  530.5 2.9 fusion.86
  533.4 1.7 fusion.83
  535.1 1.5 fusion.84
  537.3 1.6 add_convert_fusion.1
  541.7 3.5 all-to-all-start.1
  545.3 11.0 fusion.81
  556.3 9.5 all-to-all-done.1
  565.9 1.5 convert_reduce_fusion.6
  567.5 2.3 reshape.319
  569.8 1.9 multiply_reduce_fusion.9
  573.0 4.5 convolution_bitcast_fusion
  578.8 43.5 %all-reduce = (f32[4,768]{1,0:T(4,128)}, f32[768]{0:T(1024)}, f32[768]{0:T(1024)}, f32[768]{0:T(1024)}, f32[768]{0:T(1024)}, /*index=5*/f32[768]{0:T(1024)}, f32...) all-reduce(f32[4,768]{1,0:T(4,128)S(1)} %convolution_bitcast_fusion, ...), channel_id=1, replica_groups=mesh['enc'=4,'dp'=8] {'enc','dp'}, use_global_device_ids=true, to_apply=%region_17.19 | all-reduce | flops 14592 | bytes 116736 | tf_op jit(solution)/shard_map/psum | solution.py:277
  623.3 4.9 convolution_convert_fusion
  628.2 476.7 %all-reduce.4.cloned.1.call-done = (f32[2048,768]{0,1:T(8,128)}, f32[768,768]{1,0:T(8,128)}, f32[768,768]{1,0:T(8,128)}, f32[768,768]{1,0:T(8,128)}, f32[768,768...) async-done(((f32[2048,768]{0,1:T(8,128)}, f32[768,768]{1,0:T(8,128)}, f32[768,768]{1,0:T(8,128)}, f32[768,768]{1,0:T(8,128)}, f32[768,768]{1,0:T(8,128)}, ...) | async-done | bytes 34603024 | tf_op jit(solution)/shard_map/psum | solution.py:277
  1104.9 6.6 copy.84
  1111.4 3.4 copy.126
  1114.8 1.4 copy.127
  1117.3 1.4 copy.128
  1121.2 9.3 copy.130
  1130.6 3.7 copy.131
  (212 shorter events, 35.1 us)
Async XLA Ops:
  7.2 65.4 %copy-start = (bf16[416,2048]{1,0:T(8,128)(2,1)S(1)}, bf16[416,2048]{1,0:T(8,128)(2,1)}, u32[]{:S(2)}) copy-start(bf16[416,2048]{1,0:T(8,128)(2,1)} %param.34) | copy-start | bytes 5111812
  7.2 65.4 %all-gather.8.cloned.1.call-start = ((), (), s32[]{:S(2)}) async-start(), calls=%async_computation.2 | async-start | bytes 3244032 | tf_op jit(solution)/shard_map/all_gather | solution.py:73
  7.9 122.7 %all-gather.14.cloned.1.call-start = ((), (), s32[]{:S(2)}) async-start(), calls=%async_computation.5 | async-start | bytes 1216512 | tf_op jit(solution)/shard_map/all_gather | solution.py:75
  8.7 177.9 %all-gather.12.cloned.1.call-start = ((), (), s32[]{:S(2)}) async-start(), calls=%async_computation.4 | async-start | bytes 1216512 | tf_op jit(solution)/shard_map/all_gather | solution.py:74
  9.4 232.9 %all-gather.10.cloned.1.call-start = ((), (), s32[]{:S(2)}) async-start(), calls=%async_computation.3 | async-start | bytes 1216512 | tf_op jit(solution)/shard_map/all_gather | solution.py:76
  10.0 288.1 %all-gather.16.cloned.1.call-start = ((), (), s32[]{:S(2)}) async-start(), calls=%async_computation.6 | async-start | bytes 1216512 | tf_op jit(solution)/shard_map/all_gather | solution.py:77
  10.6 352.9 %all-gather.18.cloned.1.call-start = ((), (), s32[]{:S(2)}) async-start(), calls=%async_computation.7 | async-start | bytes 4866048 | tf_op jit(solution)/shard_map/all_gather | solution.py:78
  11.2 64.8 %copy-start.38 = (bf16[4,768]{1,0:T(4,128)(2,1)S(1)}, bf16[4,768]{1,0:T(4,128)(2,1)}, u32[]{:S(2)}) copy-start(bf16[4,768]{1,0:T(4,128)(2,1)} %param.40) | copy-start | bytes 18436
  11.2 64.8 %copy-start.41 = (bf16[4,416]{1,0:T(4,128)(2,1)S(1)}, bf16[4,416]{1,0:T(4,128)(2,1)}, u32[]{:S(2)}) copy-start(bf16[4,416]{1,0:T(4,128)(2,1)} %param.35) | copy-start | bytes 9988
  11.2 64.8 %copy-start.47 = (f32[768]{0:T(1024)S(1)}, f32[768]{0:T(1024)}, u32[]{:S(2)}) copy-start(f32[768]{0:T(1024)} %param.41) | copy-start | bytes 9220
  76.0 2.1 copy-start.30
  76.0 2.1 copy-start.48
  76.5 7.8 copy-start.46
  76.5 7.8 copy-start.56
  79.5 24.9 %all-to-all-start = ((bf16[32,13,768]{2,1,0:T(8,128)(2,1)}), bf16[32,13,768]{2,1,0:T(8,128)(2,1)S(1)}, u32[]{:S(2)}, u32[]{:S(2)}) async-start(bf16[32,13,768]{2,1,0:T(8,128)(2,1)} %all_to_all.14), calls=%async_computation | async-start | bytes 1572864 | tf_op jit(solution)/shard_map/all_to_all | solution.py:97
  82.9 345.9 %all-gather.20.cloned.1.call-start = ((), (), s32[]{:S(2)}) async-start(), calls=%async_computation.8 | async-start | bytes 4866048 | tf_op jit(solution)/shard_map/all_gather | solution.py:79
  88.4 16.9 %copy-start.54 = (pred[512]{0:T(512)(128)(4,1)}, pred[512]{0:T(512)(128)(4,1)S(1)}, u32[]{:S(2)}) copy-start(pred[512]{0:T(512)(128)(4,1)S(1)} %select_compare_fusion) | copy-start | bytes 1540
  88.4 16.8 %copy-start.50 = (s32[416]{0:T(512)}, s32[416]{0:T(512)S(1)}, u32[]{:S(2)}) copy-start(s32[416]{0:T(512)S(1)} %fusion.52) | copy-start | bytes 4996
  91.6 13.6 %copy-start.52 = (s32[512]{0:T(512)}, s32[512]{0:T(512)S(1)}, u32[]{:S(2)}) copy-start(s32[512]{0:T(512)S(1)} %select_add_fusion) | copy-start | bytes 6148
  106.5 24.1 %copy-start.19 = (bf16[4,256,768]{2,1,0:T(8,128)(2,1)}, bf16[4,256,768]{2,1,0:T(8,128)(2,1)S(1)}, u32[]{:S(2)}) copy-start(bf16[4,256,768]{2,1,0:T(8,128)(2,1)S(1)} %pad_maximum_fusion) | copy-start | bytes 4718596
  134.5 52.1 %copy-start.61 = (f32[768]{0:T(1024)S(1)}, f32[768]{0:T(1024)}, u32[]{:S(2)}) copy-start(f32[768]{0:T(1024)} %param.45) | copy-start | bytes 9220
  189.7 52.6 %copy-start.62 = (f32[768]{0:T(1024)S(1)}, f32[768]{0:T(1024)}, u32[]{:S(2)}) copy-start(f32[768]{0:T(1024)} %param.48) | copy-start | bytes 9220
  194.2 58.8 %copy-start.5 = (bf16[4,256,12,64]{1,0,3,2:T(4,128)(2,1)}, bf16[4,256,12,64]{1,0,3,2:T(4,128)(2,1)S(1)}, u32[]{:S(2)}) copy-start(bf16[4,256,12,64]{1,0,3,2:T(4,128)(2,1)S(1)} %reshape.313) | copy-start | bytes 4718596
  260.8 12.9 %copy-start.22 = (bf16[4,256,12,64]{1,0,3,2:T(4,128)(2,1)S(1)}, bf16[4,256,12,64]{1,0,3,2:T(4,128)(2,1)}, u32[]{:S(2)}) copy-start(bf16[4,256,12,64]{1,0,3,2:T(4,128)(2,1)} %reshape.312) | copy-start | bytes 4718596
  273.7 4.5 copy-start.8
  273.7 4.8 copy-start.27
  278.5 19.6 %copy-start.20 = (bf16[4,256,768]{2,1,0:T(8,128)(2,1)S(1)}, bf16[4,256,768]{2,1,0:T(8,128)(2,1)}, u32[]{:S(2)}) copy-start(bf16[4,256,768]{2,1,0:T(8,128)(2,1)} %copy-done.19) | copy-start | bytes 4718596
  278.5 19.6 %copy-start.63 = (f32[768]{0:T(1024)S(1)}, f32[768]{0:T(1024)}, u32[]{:S(2)}) copy-start(f32[768]{0:T(1024)} %param.50) | copy-start | bytes 9220
  301.5 61.9 %copy-start.29 = (f32[768]{0:T(1024)S(1)}, f32[768]{0:T(1024)}, u32[]{:S(2)}) copy-start(f32[768]{0:T(1024)} %param.51) | copy-start | bytes 9220
  301.5 61.9 %copy-start.34 = (f32[768]{0:T(1024)S(1)}, f32[768]{0:T(1024)}, u32[]{:S(2)}) copy-start(f32[768]{0:T(1024)} %param.52) | copy-start | bytes 9220
  301.5 61.9 %copy-start.60 = (f32[3072]{0:T(1024)S(1)}, f32[3072]{0:T(1024)}, u32[]{:S(2)}) copy-start(f32[3072]{0:T(1024)} %param.54) | copy-start | bytes 36868
  303.7 125.1 %copy-start.64 = (f32[768]{0:T(1024)S(1)}, f32[768]{0:T(1024)}, u32[]{:S(2)}) copy-start(f32[768]{0:T(1024)} %param.56) | copy-start | bytes 9220
  438.7 3.3 copy-start.49
  439.6 6.2 slice-start.6
  442.0 3.7 slice-start.7
  445.8 7.8 copy-start.15
  453.6 18.8 %copy-start.4 = (f32[1024,768]{1,0:T(8,128)S(1)}, f32[1024,768]{1,0:T(8,128)}, u32[]{:S(2)}) copy-start(f32[1024,768]{1,0:T(8,128)} %copy-done.3) | copy-start | bytes 9437188
  483.6 3.1 copy-start.9
  483.9 2.8 copy-start.59
  489.3 4.1 copy-start.28
  493.4 7.3 copy-start.23
  493.4 7.4 copy-start.25
  493.4 16.3 %slice-start = ((s8[12582912]{0:T(1024)(128)(4,1)}), s8[4194304]{0:T(1024)(128)(4,1)S(1)}, s32[]{:S(2)}) async-start(s8[12582912]{0:T(1024)(128)(4,1)} %bitcast.136), calls=%async_computation.10 | async-start | bytes 8388608
  493.4 16.3 %slice-start.1 = ((s8[12582912]{0:T(1024)(128)(4,1)}), s8[4194304]{0:T(1024)(128)(4,1)S(1)}, s32[]{:S(2)}) async-start(s8[12582912]{0:T(1024)(128)(4,1)} %bitcast.136), calls=%async_computation.11 | async-start | bytes 8388608
  500.8 8.9 slice-start.2
  509.7 6.9 copy-start.6
  516.7 2.0 copy-start.7
  530.5 2.9 copy-start.58
  535.1 1.9 copy-start.10
  535.1 2.2 copy-start.26
  541.7 24.1 %all-to-all-start.1 = ((bf16[32,13,768]{2,1,0:T(8,128)(2,1)}), bf16[32,13,768]{2,1,0:T(8,128)(2,1)}, u32[]{:S(2)}, u32[]{:S(2)}) async-start(bf16[32,13,768]{2,1,0:T(8,128)(2,1)} %all_to_all.17), calls=%async_computation.1 | async-start | bytes 1572864 | tf_op jit(solution)/shard_map/all_to_all | solution.py:242
  545.2 20.6 %copy-start.31 = (f32[768]{0:T(1024)S(1)}, f32[768]{0:T(1024)}, u32[]{:S(2)}) copy-start(f32[768]{0:T(1024)} %param.42) | copy-start | bytes 9220
  545.3 24.5 %copy-start.33 = (f32[416]{0:T(512)S(1)}, f32[416]{0:T(512)}, u32[]{:S(2)}) copy-start(f32[416]{0:T(512)} %copy-done.32) | copy-start | bytes 4996
  545.3 24.5 %copy-start.37 = (f32[416]{0:T(512)S(1)}, f32[416]{0:T(512)}, u32[]{:S(2)}) copy-start(f32[416]{0:T(512)} %copy-done.36) | copy-start | bytes 4996
  545.3 559.6 %all-reduce.4.cloned.1.call-start = ((), (), s32[]{:S(2)}) async-start(), calls=%async_computation.9 | async-start | bytes 69206016 | tf_op jit(solution)/shard_map/psum | solution.py:277
  556.3 13.5 %copy-start.2 = (f32[416,768]{1,0:T(8,128)S(1)}, f32[416,768]{1,0:T(8,128)}, u32[]{:S(2)}) copy-start(f32[416,768]{1,0:T(8,128)} %copy-done.1) | copy-start | bytes 3833860
  569.8 1.9 copy-start.11
  577.6 44.8 %copy-start.39 = (bf16[4,768]{1,0:T(4,128)(2,1)S(1)}, bf16[4,768]{1,0:T(4,128)(2,1)}, u32[]{:S(2)}) copy-start(bf16[4,768]{1,0:T(4,128)(2,1)} %param.40) | copy-start | bytes 18436
  1111.4 3.4 copy-start.18
  1114.8 2.5 copy-start.17
  1117.3 2.5 copy-start.16
  1119.8 10.7 slice-start.3
  1121.2 9.3 slice-start.4
  1121.2 9.3 slice-start.5
  (19 other events, 23.1 us)
Sparse Core Ops, SparseCore 0:
  10.9 61.6 all-gather.7
  75.5 55.1 all-gather.13
  133.6 52.9 all-gather.11
  189.3 52.9 all-gather.9
  245.1 52.9 all-gather.15
  300.8 62.5 all-gather.17
  366.3 62.4 all-gather.19
  577.7 527.0 all-reduce.3
where the time goes:
time: 1150 us; the launch traced here: 1140 us
  waiting for transfers between devices  788 us (69%)
  matrix products  173 us (15%)
  local copies, waits for them, and re-layouts  74.1 us (6%)
  blocking collectives  43.5 us (4%)
  other arithmetic  39.3 us (3%)
  between operations  16 us (1%)
    psum x1, waiting for transfers between devices, body(): lax.psum((grad_w_img, grad_w_box, grad_b_img, grad_g_reg, grad_beta_reg,...  477 us
    all_gather x1, waiting for transfers between devices, body(): lax.all_gather(w_img, ('enc', 'dp'), axis=0, tiled=True)  61.4 us
    all_gather x1, waiting for transfers between devices, body(): lax.all_gather(w_up, ('enc', 'dp'), axis=0, tiled=True)  59.7 us
    all_gather x1, waiting for transfers between devices, body(): lax.all_gather(w_value, ('enc', 'dp'), axis=0, tiled=True)  48.1 us
    all_gather x1, waiting for transfers between devices, body(): lax.all_gather(w_query, ('enc', 'dp'), axis=0, tiled=True)  48 us
    psum x1, blocking collectives, body(): lax.psum((grad_w_img, grad_w_box, grad_b_img, grad_g_reg, grad_beta_reg,...  43.5 us
    unnamed x158, local copies, waits for them, and re-layouts  43 us
    dot_general x7, matrix products, back_product(): jnp.einsum('rb,ab->ra', row_grad, weight, preferred_element_type=jnp.floa...  41 us
  transfers between devices with their start and end apart: 10, of which 10 were waited for; matrix products, arithmetic and copies ran while one was open for 11% of the time, Pallas kernels for 0%

commit v1 on v0

--- a/solution.py
+++ b/solution.py
@@ -1,3 +1,4 @@
+import functools
 import jax
 import jax.numpy as jnp
 from jax import lax
@@ -5,6 +6,24 @@
 
 HEADS = 12
 epsilon = 1e-05
+
+
+def view_edges(arr_in, axis_key):
+    formed = lax.axis_size(axis_key)
+    tall, carry = (formed, lax.axis_index(axis_key))
+    block_next, local_now = (arr_in, 1)
+    while local_now < tall:
+        m_next = lax.ppermute(
+            block_next, axis_key, list(map(lambda rr: (rr, rr ^ local_now), range(tall)))
+        )
+        local_out = jnp.concatenate([block_next, m_next], axis=0)
+        current_arr = jnp.concatenate([m_next, block_next], axis=0)
+        block_next = jnp.where(carry & local_now == 0, local_out, current_arr)
+        local_now = 2 * local_now
+    return block_next
+
+
+mix_copies = functools.partial(view_edges, axis_key=("enc", "dp"))
 
 
 def normalize(values, gain_vec, shift_vec):
@@ -76,7 +95,7 @@
         lax.all_gather(w_value, ("enc", "dp"), axis=0, tiled=True),
         lax.all_gather(w_out, ("enc", "dp"), axis=0, tiled=True),
         lax.all_gather(w_up, ("enc", "dp"), axis=0, tiled=True),
-        lax.all_gather(w_down, ("enc", "dp"), axis=0, tiled=True),
+        mix_copies(w_down),
     )
     device_count = lax.axis_size(("enc", "dp"))
     seq_count = caption_count.shape[0]

time: 1150 us -> 1220 us (1.061)
  waiting for transfers between devices: 788 us -> 843 us
    all_to_all x1, waiting for transfers between devices: 12.7 us -> 59.9 us  [body(): lax.all_to_all(encoded.astype(jnp.bfloat16), ('enc', 'dp'), split_axis=0,...]
    all_gather x1, waiting for transfers between devices: 24.1 us -> 65.5 us  [body(): lax.all_gather(w_key, ('enc', 'dp'), axis=0, tiled=True)]
    all_gather x1 -> x0, waiting for transfers between devices: 27.3 us -> none  [body(): lax.all_gather(w_down, ('enc', 'dp'), axis=0, tiled=True)]
    all_gather x1, waiting for transfers between devices: 61.4 us -> 34.1 us  [body(): lax.all_gather(w_img, ('enc', 'dp'), axis=0, tiled=True)]
    ppermute x0 -> x5, waiting for transfers between devices: none -> 21.7 us  [view_edges(): lax.ppermute(block_next, axis_key, list(map(lambda rr: (rr, rr ^ local_no...]
    unnamed x158 -> x154, local copies, waits for them, and re-layouts: 43 us -> 42.9 us
  transfers between devices with their start and end apart: 10 -> 14, of which waited for: 10 -> 12; matrix products, arithmetic and copies ran while one was open for 11% -> 11% of each run, Pallas kernels for 0% -> 0%
where the time goes in v1:
time: 1220 us
  waiting for transfers between devices  843 us (69%)
  matrix products  174 us (14%)
  local copies, waits for them, and re-layouts  75.2 us (6%)
  other arithmetic  44.1 us (4%)
  blocking collectives  43.5 us (4%)
  starting transfers between devices  19.8 us (2%)
  between operations  15.9 us (1%)
    psum x1, waiting for transfers between devices, body(): lax.psum((grad_w_img, grad_w_box, grad_b_img, grad_g_reg, grad_beta_reg,...  477 us
    all_gather x1, waiting for transfers between devices, body(): lax.all_gather(w_key, ('enc', 'dp'), axis=0, tiled=True)  65.5 us
    all_to_all x1, waiting for transfers between devices, body(): lax.all_to_all(encoded.astype(jnp.bfloat16), ('enc', 'dp'), split_axis=0,...  59.9 us
    all_gather x1, waiting for transfers between devices, body(): lax.all_gather(w_up, ('enc', 'dp'), axis=0, tiled=True)  59.7 us
    all_gather x1, waiting for transfers between devices, body(): lax.all_gather(w_value, ('enc', 'dp'), axis=0, tiled=True)  48.1 us
    all_gather x1, waiting for transfers between devices, body(): lax.all_gather(w_query, ('enc', 'dp'), axis=0, tiled=True)  48 us
    psum x1, blocking collectives, body(): lax.psum((grad_w_img, grad_w_box, grad_b_img, grad_g_reg, grad_beta_reg,...  43.5 us
    unnamed x154, local copies, waits for them, and re-layouts  42.9 us
  transfers between devices with their start and end apart: 14, of which 12 were waited for; matrix products, arithmetic and copies ran while one was open for 11% of the time, Pallas kernels for 0%

profile of v1, /device:TPU:0, one launch (start us, length us, event | category | flops | bytes accessed | tf_op | source)
XLA Modules:
  0.0 1215.7 jit_solution(16083378988239240381)
XLA Ops:
  13.4 2.9 collective-permute-start.1
  16.3 7.3 collective-permute-done.1
  23.8 1.8 collective-permute-start.2
  25.7 13.2 %collective-permute-done.2 = bf16[384,768]{1,0:T(8,128)(2,1)} collective-permute-done((bf16[384,768]{1,0:T(8,128)(2,1)S(1)}, bf16[384,768]{1,0:T(8,128)(2,1)}, u32[]{:S(2)}, u32[]{:S(2)}) %collective-permute-start.2) | collective-permute-done | bytes 589856 | tf_op jit(solution)/shard_map/ppermute | solution.py:16
  38.9 1.6 maximum_select_fusion.2
  42.1 34.1 %all-gather.7.cloned.1.call-done = bf16[2048,768]{1,0:T(8,128)(2,1)} async-done(((bf16[64,768]{1,0:T(8,128)(2,1)}), bf16[2048,768]{1,0:T(8,128)(2,1)}) %all-gather.7.cloned.1.call-update) | async-done | bytes 3145744 | tf_op jit(solution)/shard_map/all_gather | solution.py:92
  76.2 3.4 fusion.84
  83.1 6.4 all-to-all-start
  91.7 2.6 select_compare_fusion
  94.9 2.6 select_add_fusion
  97.5 2.9 maximum_select_fusion.1
  100.5 2.8 collective-permute-start.4
  103.3 59.9 %all-to-all-done = bf16[32,13,768]{2,1,0:T(8,128)(2,1)} async-done(((bf16[32,13,768]{2,1,0:T(8,128)(2,1)}), bf16[32,13,768]{2,1,0:T(8,128)(2,1)}, u32[]{:S(2)}, u32[]{:S(2)}) %all-to-all-start) | async-done | bytes 639008 | tf_op jit(solution)/shard_map/all_to_all | solution.py:116
  166.5 65.5 %all-gather.13.cloned.1.call-done = bf16[768,768]{1,0:T(8,128)(2,1)} async-done(((bf16[24,768]{1,0:T(8,128)(2,1)}), bf16[768,768]{1,0:T(8,128)(2,1)}) %all-gather.13.cloned.1.call-update) | async-done | bytes 1179664 | tf_op jit(solution)/shard_map/all_gather | solution.py:94
  232.1 3.8 convolution_convert_fusion.2
  235.9 1.7 copy.66
  237.6 2.4 reshape.314
  240.0 48.0 %all-gather.11.cloned.1.call-done = bf16[768,768]{1,0:T(8,128)(2,1)} async-done(((bf16[24,768]{1,0:T(8,128)(2,1)}), bf16[768,768]{1,0:T(8,128)(2,1)}) %all-gather.11.cloned.1.call-update) | async-done | bytes 1179664 | tf_op jit(solution)/shard_map/all_gather | solution.py:93
  288.0 3.1 add_convert_fusion.3
  291.1 1.6 copy.65
  292.7 2.9 reshape.313
  295.6 48.1 %all-gather.9.cloned.1.call-done = bf16[768,768]{1,0:T(8,128)(2,1)} async-done(((bf16[24,768]{1,0:T(8,128)(2,1)}), bf16[768,768]{1,0:T(8,128)(2,1)}) %all-gather.9.cloned.1.call-update) | async-done | bytes 1179664 | tf_op jit(solution)/shard_map/all_gather | solution.py:95
  343.7 4.3 add_convert_fusion.4
  348.0 2.6 copy.64
  350.6 3.9 reshape.312
  354.4 7.8 fusion.39
  362.2 12.9 %fusion.80 = (f32[4,12,256]{2,1,0:T(8,128)S(1)}, f32[4,12,256,256]{2,3,1,0:T(8,128)S(1)}) fusion(f32[4,12,256,256]{2,3,1,0:T(8,128)} %fusion.39, pred[4,256]{1,0:T(4,128)(4,1)S(1)} %get-tuple-element.137), kind=kOutput, calls=%fused_computation.170 | output fusion | flops 18874624 | bytes 25216000 | tf_op jit(solution)/shard_map/sub | solution.py:169
  376.2 3.4 copy-done.8
  382.6 16.9 %all-gather.15.cloned.1.call-done = bf16[768,768]{1,0:T(8,128)(2,1)} async-done(((bf16[24,768]{1,0:T(8,128)(2,1)}), bf16[768,768]{1,0:T(8,128)(2,1)}) %all-gather.15.cloned.1.call-update) | async-done | bytes 1179664 | tf_op jit(solution)/shard_map/all_gather | solution.py:96
  399.5 3.4 fusion.81
  403.0 1.6 copy-done.3
  405.1 59.7 %all-gather.17.cloned.1.call-done = bf16[768,3072]{1,0:T(8,128)(2,1)} async-done(((bf16[24,3072]{1,0:T(8,128)(2,1)}), bf16[768,3072]{1,0:T(8,128)(2,1)}) %all-gather.17.cloned.1.call-update) | async-done | bytes 4718608 | tf_op jit(solution)/shard_map/all_gather | solution.py:97
  464.8 37.6 %multiply_convert_fusion.1 = (bf16[1024,3072]{1,0:T(8,128)(2,1)S(1)}, f32[1024,3072]{1,0:T(8,128)}, f32[1024,3072]{1,0:T(8,128)}) fusion(f32[3072]{0:T(1024)S(1)} %copy-done.60, bf16[768,3072]{1,0:T(8,128)(2,1)} %all-gather.17.cloned.1.call-done, f32[1024,768]{1,0:T(8,128)} %copy-done.3, f32[768]{0:T(1024)S(1)} %copy-done.35, f32[768]{0:T(1024)S(1)} %copy-done.30, ...), kind=kOutput, calls=%fused_computation.7 | convolution fusion | flops 5043388416 | bytes 39348224 | tf_op jit(solution)/shard_map/dot_general | solution.py:184
  502.5 10.8 fusion.82
  514.8 2.4 multiply_reduce_fusion.1
  517.2 2.7 convert_reduce_fusion.1
  519.9 7.8 fusion.70
  527.7 17.3 %convert_reduce_fusion = (f32[3072]{0:T(1024)S(1)}, bf16[1024,3072]{1,0:T(8,128)(2,1)S(1)}) fusion(f32[1024,3072]{1,0:T(8,128)} %get-tuple-element.132, bf16[1536,768]{1,0:T(8,128)(2,1)} %collective-permute-done.4, bf16[1536,768]{1,0:T(8,128)(2,1)} %maximum_select_fusion.1, pred[]{:T(512)S(6)} %eq.36, f32[1024,768]{1,0:T(8,128)} %copy-done.16, ...), kind=kOutput, calls=%fused_computation.3 | convolution fusion | flops 4907332608 | bytes 39346176 | tf_op jit(solution)/shard_map/rb,ab->ra/dot_general | solution.py:55
  545.0 11.6 multiply_reduce_fusion.2
  558.1 2.8 fusion.67
  560.9 2.6 convolution_convert_fusion.1
  563.5 1.7 copy.72
  565.2 2.4 reshape.315
  567.6 7.3 convert_reduce_fusion.3
  575.0 8.9 multiply_reduce_fusion
  583.9 6.9 multiply_convert_fusion
  590.9 2.0 fusion.31
  595.8 2.9 fusion.89
  601.9 2.9 fusion.87
  604.7 2.9 fusion.88
  607.6 1.9 fusion.85
  616.1 3.5 all-to-all-start.1
  619.7 11.0 fusion.83
  630.7 9.5 all-to-all-done.1
  641.9 2.3 reshape.319
  644.2 1.9 multiply_reduce_fusion.9
  647.4 4.5 convolution_bitcast_fusion
  653.2 43.5 %all-reduce = (f32[4,768]{1,0:T(4,128)}, f32[768]{0:T(1024)}, f32[768]{0:T(1024)}, f32[768]{0:T(1024)}, f32[768]{0:T(1024)}, /*index=5*/f32[768]{0:T(1024)}, f32...) all-reduce(f32[4,768]{1,0:T(4,128)S(1)} %convolution_bitcast_fusion, ...), channel_id=1, replica_groups=mesh['enc'=4,'dp'=8] {'enc','dp'}, use_global_device_ids=true, to_apply=%region_17.19 | all-reduce | flops 14592 | bytes 116736 | tf_op jit(solution)/shard_map/psum | solution.py:296
  697.6 4.9 convolution_convert_fusion
  702.5 476.8 %all-reduce.4.cloned.1.call-done = (f32[2048,768]{0,1:T(8,128)}, f32[768,768]{1,0:T(8,128)}, f32[768,768]{1,0:T(8,128)}, f32[768,768]{1,0:T(8,128)}, f32[768,768...) async-done(((f32[2048,768]{0,1:T(8,128)}, f32[768,768]{1,0:T(8,128)}, f32[768,768]{1,0:T(8,128)}, f32[768,768]{1,0:T(8,128)}, f32[768,768]{1,0:T(8,128)}, ...) | async-done | bytes 34603024 | tf_op jit(solution)/shard_map/psum | solution.py:296
  1179.3 6.6 copy.84
  1185.8 3.4 copy.126
  1195.6 9.3 copy.130
  1205.0 3.7 copy.131
  (218 shorter events, 48.4 us)
Async XLA Ops:
  7.2 69.0 %copy-start = (bf16[416,2048]{1,0:T(8,128)(2,1)S(1)}, bf16[416,2048]{1,0:T(8,128)(2,1)}, u32[]{:S(2)}) copy-start(bf16[416,2048]{1,0:T(8,128)(2,1)} %param.34) | copy-start | bytes 5111812
  7.2 69.0 %all-gather.7.cloned.1.call-start = ((), (), s32[]{:S(2)}) async-start(), calls=%async_computation.2 | async-start | bytes 3244032 | tf_op jit(solution)/shard_map/all_gather | solution.py:92
  7.9 224.1 %all-gather.13.cloned.1.call-start = ((), (), s32[]{:S(2)}) async-start(), calls=%async_computation.5 | async-start | bytes 1216512 | tf_op jit(solution)/shard_map/all_gather | solution.py:94
  8.7 279.3 %all-gather.11.cloned.1.call-start = ((), (), s32[]{:S(2)}) async-start(), calls=%async_computation.4 | async-start | bytes 1216512 | tf_op jit(solution)/shard_map/all_gather | solution.py:93
  9.4 334.3 %all-gather.9.cloned.1.call-start = ((), (), s32[]{:S(2)}) async-start(), calls=%async_computation.3 | async-start | bytes 1216512 | tf_op jit(solution)/shard_map/all_gather | solution.py:95
  10.0 389.5 %all-gather.15.cloned.1.call-start = ((), (), s32[]{:S(2)}) async-start(), calls=%async_computation.6 | async-start | bytes 1216512 | tf_op jit(solution)/shard_map/all_gather | solution.py:96
  10.6 454.2 %all-gather.17.cloned.1.call-start = ((), (), s32[]{:S(2)}) async-start(), calls=%async_computation.7 | async-start | bytes 4866048 | tf_op jit(solution)/shard_map/all_gather | solution.py:97
  10.6 1.7 collective-permute-start
  13.4 10.2 collective-permute-start.1
  23.8 15.0 %collective-permute-start.2 = (bf16[384,768]{1,0:T(8,128)(2,1)S(1)}, bf16[384,768]{1,0:T(8,128)(2,1)}, u32[]{:S(2)}, u32[]{:S(2)}) collective-permute-start(bf16[384,768]{1,0:T(8,128)(2,1)S(1)} %maximum_select_fusion.5), channel_id=1, source_target_pairs={{0,4},{1,5},{2,6},{3,7},{4,0},{5,1},{6,2},{7,3},{8,12},{9,13},{10,... | collective-permute-start | bytes 1769480 | tf_op jit(solution)/shard_map/ppermute | solution.py:16
  40.5 39.1 %copy-start.39 = (bf16[4,768]{1,0:T(4,128)(2,1)S(1)}, bf16[4,768]{1,0:T(4,128)(2,1)}, u32[]{:S(2)}) copy-start(bf16[4,768]{1,0:T(4,128)(2,1)} %param.40) | copy-start | bytes 18436
  40.5 39.1 %copy-start.42 = (bf16[4,416]{1,0:T(4,128)(2,1)S(1)}, bf16[4,416]{1,0:T(4,128)(2,1)}, u32[]{:S(2)}) copy-start(bf16[4,416]{1,0:T(4,128)(2,1)} %param.35) | copy-start | bytes 9988
  40.5 39.1 %copy-start.47 = (f32[768]{0:T(1024)S(1)}, f32[768]{0:T(1024)}, u32[]{:S(2)}) copy-start(f32[768]{0:T(1024)} %param.41) | copy-start | bytes 9220
  40.5 57.0 %collective-permute-start.3 = (bf16[768,768]{1,0:T(8,128)(2,1)S(1)}, bf16[768,768]{1,0:T(8,128)(2,1)}, u32[]{:S(2)}, u32[]{:S(2)}) collective-permute-start(bf16[768,768]{1,0:T(8,128)(2,1)S(1)} %maximum_select_fusion.2), channel_id=1, source_target_pairs={{0,8},{1,9},{2,10},{3,11},{4,12},{5,13},{6,14},{7,15},{8,0},{9,1},... | collective-permute-start | bytes 3538952 | tf_op jit(solution)/shard_map/ppermute | solution.py:16
  79.6 2.2 copy-start.31
  79.6 2.1 copy-start.48
  80.1 9.4 copy-start.46
  80.2 9.4 copy-start.56
  83.1 80.1 %all-to-all-start = ((bf16[32,13,768]{2,1,0:T(8,128)(2,1)}), bf16[32,13,768]{2,1,0:T(8,128)(2,1)}, u32[]{:S(2)}, u32[]{:S(2)}) async-start(bf16[32,13,768]{2,1,0:T(8,128)(2,1)} %all_to_all.14), calls=%async_computation | async-start | bytes 1572864 | tf_op jit(solution)/shard_map/all_to_all | solution.py:116
  94.3 71.0 %copy-start.54 = (pred[512]{0:T(512)(128)(4,1)}, pred[512]{0:T(512)(128)(4,1)S(1)}, u32[]{:S(2)}) copy-start(pred[512]{0:T(512)(128)(4,1)S(1)} %select_compare_fusion) | copy-start | bytes 1540
  94.3 70.9 %copy-start.50 = (s32[416]{0:T(512)}, s32[416]{0:T(512)S(1)}, u32[]{:S(2)}) copy-start(s32[416]{0:T(512)S(1)} %fusion.52) | copy-start | bytes 4996
  97.5 67.7 %copy-start.52 = (s32[512]{0:T(512)}, s32[512]{0:T(512)S(1)}, u32[]{:S(2)}) copy-start(s32[512]{0:T(512)S(1)} %select_add_fusion) | copy-start | bytes 6148
  100.5 402.0 %collective-permute-start.4 = (bf16[1536,768]{1,0:T(8,128)(2,1)}, bf16[1536,768]{1,0:T(8,128)(2,1)}, u32[]{:S(2)}, u32[]{:S(2)}) collective-permute-start(bf16[1536,768]{1,0:T(8,128)(2,1)} %maximum_select_fusion.1), channel_id=1, source_target_pairs={{0,16},{1,17},{2,18},{3,19},{4,20},{5,21},{6,22},{7,23},{8,24},{9,... | collective-permute-start | bytes 7077896 | tf_op jit(solution)/shard_map/ppermute | solution.py:16
  166.5 65.6 %copy-start.20 = (bf16[4,256,768]{2,1,0:T(8,128)(2,1)}, bf16[4,256,768]{2,1,0:T(8,128)(2,1)S(1)}, u32[]{:S(2)}) copy-start(bf16[4,256,768]{2,1,0:T(8,128)(2,1)S(1)} %pad_maximum_fusion) | copy-start | bytes 4718596
  235.9 52.1 %copy-start.61 = (f32[768]{0:T(1024)S(1)}, f32[768]{0:T(1024)}, u32[]{:S(2)}) copy-start(f32[768]{0:T(1024)} %param.45) | copy-start | bytes 9220
  291.1 52.6 %copy-start.62 = (f32[768]{0:T(1024)S(1)}, f32[768]{0:T(1024)}, u32[]{:S(2)}) copy-start(f32[768]{0:T(1024)} %param.48) | copy-start | bytes 9220
  295.6 58.8 %copy-start.5 = (bf16[4,256,12,64]{1,0,3,2:T(4,128)(2,1)}, bf16[4,256,12,64]{1,0,3,2:T(4,128)(2,1)S(1)}, u32[]{:S(2)}) copy-start(bf16[4,256,12,64]{1,0,3,2:T(4,128)(2,1)S(1)} %reshape.313) | copy-start | bytes 4718596
  362.2 12.9 %copy-start.23 = (bf16[4,256,12,64]{1,0,3,2:T(4,128)(2,1)S(1)}, bf16[4,256,12,64]{1,0,3,2:T(4,128)(2,1)}, u32[]{:S(2)}) copy-start(bf16[4,256,12,64]{1,0,3,2:T(4,128)(2,1)} %reshape.312) | copy-start | bytes 4718596
  375.1 4.5 copy-start.8
  375.1 4.8 copy-start.28
  379.9 19.6 %copy-start.21 = (bf16[4,256,768]{2,1,0:T(8,128)(2,1)S(1)}, bf16[4,256,768]{2,1,0:T(8,128)(2,1)}, u32[]{:S(2)}) copy-start(bf16[4,256,768]{2,1,0:T(8,128)(2,1)} %copy-done.20) | copy-start | bytes 4718596
  379.9 19.6 %copy-start.63 = (f32[768]{0:T(1024)S(1)}, f32[768]{0:T(1024)}, u32[]{:S(2)}) copy-start(f32[768]{0:T(1024)} %param.50) | copy-start | bytes 9220
  402.9 61.9 %copy-start.30 = (f32[768]{0:T(1024)S(1)}, f32[768]{0:T(1024)}, u32[]{:S(2)}) copy-start(f32[768]{0:T(1024)} %param.51) | copy-start | bytes 9220
  402.9 61.9 %copy-start.35 = (f32[768]{0:T(1024)S(1)}, f32[768]{0:T(1024)}, u32[]{:S(2)}) copy-start(f32[768]{0:T(1024)} %param.52) | copy-start | bytes 9220
  402.9 61.9 %copy-start.60 = (f32[3072]{0:T(1024)S(1)}, f32[3072]{0:T(1024)}, u32[]{:S(2)}) copy-start(f32[3072]{0:T(1024)} %param.54) | copy-start | bytes 36868
  405.1 97.4 %copy-start.64 = (f32[768]{0:T(1024)S(1)}, f32[768]{0:T(1024)}, u32[]{:S(2)}) copy-start(f32[768]{0:T(1024)} %param.56) | copy-start | bytes 9220
  464.8 37.7 %copy-start.4 = (f32[1024,768]{1,0:T(8,128)S(1)}, f32[1024,768]{1,0:T(8,128)}, u32[]{:S(2)}) copy-start(f32[1024,768]{1,0:T(8,128)} %copy-done.3) | copy-start | bytes 9437188
  513.9 3.3 copy-start.49
  519.9 7.8 copy-start.16
  545.0 11.6 copy-start.12
  557.8 3.1 copy-start.9
  558.1 2.8 copy-start.59
  563.5 4.1 copy-start.29
  567.6 7.3 copy-start.24
  567.6 7.4 copy-start.26
  567.6 16.3 %slice-start = ((s8[12582912]{0:T(1024)(128)(4,1)}), s8[4194304]{0:T(1024)(128)(4,1)S(1)}, s32[]{:S(2)}) async-start(s8[12582912]{0:T(1024)(128)(4,1)} %bitcast.134), calls=%async_computation.9 | async-start | bytes 8388608
  567.6 16.3 %slice-start.1 = ((s8[12582912]{0:T(1024)(128)(4,1)}), s8[4194304]{0:T(1024)(128)(4,1)S(1)}, s32[]{:S(2)}) async-start(s8[12582912]{0:T(1024)(128)(4,1)} %bitcast.134), calls=%async_computation.10 | async-start | bytes 8388608
  575.0 8.9 slice-start.2
  583.9 7.0 copy-start.6
  604.7 2.9 copy-start.58
  609.5 2.2 copy-start.27
  616.1 24.1 %all-to-all-start.1 = ((bf16[32,13,768]{2,1,0:T(8,128)(2,1)}), bf16[32,13,768]{2,1,0:T(8,128)(2,1)}, u32[]{:S(2)}, u32[]{:S(2)}) async-start(bf16[32,13,768]{2,1,0:T(8,128)(2,1)} %all_to_all.17), calls=%async_computation.1 | async-start | bytes 1572864 | tf_op jit(solution)/shard_map/all_to_all | solution.py:261
  619.7 20.6 %copy-start.32 = (f32[768]{0:T(1024)S(1)}, f32[768]{0:T(1024)}, u32[]{:S(2)}) copy-start(f32[768]{0:T(1024)} %param.42) | copy-start | bytes 9220
  619.7 24.5 %copy-start.34 = (f32[416]{0:T(512)S(1)}, f32[416]{0:T(512)}, u32[]{:S(2)}) copy-start(f32[416]{0:T(512)} %copy-done.33) | copy-start | bytes 4996
  619.7 24.5 %copy-start.38 = (f32[416]{0:T(512)S(1)}, f32[416]{0:T(512)}, u32[]{:S(2)}) copy-start(f32[416]{0:T(512)} %copy-done.37) | copy-start | bytes 4996
  619.7 559.6 %all-reduce.4.cloned.1.call-start = ((), (), s32[]{:S(2)}) async-start(), calls=%async_computation.8 | async-start | bytes 69206016 | tf_op jit(solution)/shard_map/psum | solution.py:296
  630.7 13.5 %copy-start.2 = (f32[416,768]{1,0:T(8,128)S(1)}, f32[416,768]{1,0:T(8,128)}, u32[]{:S(2)}) copy-start(f32[416,768]{1,0:T(8,128)} %copy-done.1) | copy-start | bytes 3833860
  652.0 44.7 %copy-start.40 = (bf16[4,768]{1,0:T(4,128)(2,1)S(1)}, bf16[4,768]{1,0:T(4,128)(2,1)}, u32[]{:S(2)}) copy-start(bf16[4,768]{1,0:T(4,128)(2,1)} %param.40) | copy-start | bytes 18436
  1185.8 3.4 copy-start.19
  1189.2 2.5 copy-start.18
  1191.7 2.5 copy-start.17
  1194.2 10.7 slice-start.3
  1195.6 9.3 slice-start.4
  1195.6 9.3 slice-start.5
  (21 other events, 27.7 us)
Sparse Core Ops, SparseCore 0:
  10.9 65.2 all-gather.6
  79.1 152.8 all-gather.12
  235.0 52.9 all-gather.10
  290.7 52.9 all-gather.8
  346.5 52.9 all-gather.14
  402.2 62.5 all-gather.16
  652.1 527.0 all-reduce.3
